TPU v7x, 32 devices: a whole 2x2x4 slice. The times are simulated.
32 devices in a mesh: grp: 4 (over z), mem: 8 (over y, x, core).
Axes of the slice: x: 2, y: 2, z: 4, core: 2. Of those that a mesh axis runs over, the one named last changes fastest.
Arguments:
- basis: float32 [20, 2048, 128], P(None, ('grp', 'mem'))
- precond: bfloat16 [2048, 128, 128], P(('grp', 'mem'))
- leaf_rows: float32 [1024, 128], P(('grp', 'mem')), may hold values from -6 to 6
- leaf_fiber: int32 [1024], P(('grp', 'mem')), may hold values from 0 to 63
- strad_rows: float32 [1024, 128], P(('grp', 'mem')), may hold values from -6 to 6
- strad_fiber: int32 [1024], P(('grp', 'mem')), may hold values from 0 to 63
- strad_count: int32 [32, 4], P(('grp', 'mem')), may hold values from 0 to 8, as said below
Outputs:
- coeffs: float32 [21], replicated
- next_vector: float32 [2048, 128], P(('grp', 'mem'))
Inputs may be any that keep to these rules, and one draw needn't show every extreme that they name: `leaf_fiber`: a destination fiber within the destination device. `strad_fiber`: a fiber of the receiving device. The first strad_count slots of a block are live, the rest are not read; some device fills a block.
All inputs are finite; a program needn't handle non-finite values.
Results may differ from a plain program's by a relative error of at most 0.0011.
Values sent between devices are 32-bit elements; how exact they have to be, the bound alone decides.
A program may use at most 64 MiB of HBM per device.

v0:
```python
import jax
import jax.numpy as jnp
from jax import lax
from jax.sharding import PartitionSpec as P

EPS = 1e-06


def local(basis, precond, leaf_rows, leaf_fiber, strad_rows, strad_fiber, strad_count):
    groups = lax.axis_size("grp")
    members = lax.axis_size("mem")
    krylov, fibers_here, width = basis.shape
    fiber_index = jnp.arange(fibers_here, dtype=jnp.int32)
    arrived, arrived_ids = (
        lax.all_to_all(leaf_rows, "mem", split_axis=0, concat_axis=0, tiled=True),
        lax.all_to_all(
            leaf_fiber.astype(jnp.float32), "mem", split_axis=0, concat_axis=0, tiled=True
        ),
    )
    select = (fiber_index[:, None] == arrived_ids.astype(jnp.int32)[None, :]).astype(jnp.float32)
    far_field = jnp.dot(
        select, arrived, precision=lax.Precision.HIGHEST, preferred_element_type=jnp.float32
    )
    strad_slots = strad_rows.shape[0] // groups
    keeping = (jnp.arange(strad_slots, dtype=jnp.int32)[None, :] < strad_count[0][:, None]).reshape(
        -1
    )
    outgoing = strad_rows * keeping[:, None].astype(jnp.float32)
    incoming = lax.all_to_all(outgoing, "grp", split_axis=0, concat_axis=0, tiled=True)
    select_near = (fiber_index[:, None] == strad_fiber[None, :]).astype(jnp.float32)
    near_field = jnp.dot(
        select_near, incoming, precision=lax.Precision.HIGHEST, preferred_element_type=jnp.float32
    )
    field = (basis[krylov - 1] + far_field + near_field).astype(jnp.bfloat16)
    applied = jnp.einsum("fij,fj->fi", precond, field, preferred_element_type=jnp.float32)
    total = float(fibers_here * width * groups * members)
    local_coef = jnp.einsum("kfi,fi->k", basis, applied, precision=lax.Precision.HIGHEST)
    gram_local = jnp.einsum("kfi,lfi->kl", basis, basis, precision=lax.Precision.HIGHEST)
    coef_sum, square_sum, gram_sum = lax.psum(
        (local_coef, jnp.sum(applied * applied), gram_local), ("grp", "mem")
    )
    coef = coef_sum / total
    gram = gram_sum / total
    residual = applied - jnp.einsum("k,kfi->fi", coef, basis, precision=lax.Precision.HIGHEST)
    projected = jnp.dot(gram, coef, precision=lax.Precision.HIGHEST)
    square = square_sum / total - 2.0 * jnp.sum(coef * coef) + jnp.sum(coef * projected)
    beta = jnp.sqrt(square + EPS)
    return (jnp.concatenate([coef, beta[None]]), residual / beta)


def solution(mesh):
    return jax.shard_map(
        local,
        mesh=mesh,
        in_specs=(
            P(None, ("grp", "mem"), None),
            P(("grp", "mem"), None, None),
            P(("grp", "mem"), None),
            P(("grp", "mem")),
            P(("grp", "mem"), None),
            P(("grp", "mem")),
            P(("grp", "mem"), None),
        ),
        out_specs=(P(), P(("grp", "mem"), None)),
        check_vma=False,
    )
```

profile of v0, /device:TPU:0, one launch (start us, length us, event | category | flops | bytes accessed | tf_op | source)
XLA Modules:
  0.0 79.5 jit_solution(3475346898591158441)
XLA Ops:
  0.6 0.0 copy-start
  0.6 0.0 copy-start.1
  0.7 0.8 %convert_element_type.29 = f32[32]{0:T(128)S(1)} convert(s32[32]{0:T(128)} %param.10) | non-fusion elementwise | flops 32 | bytes 256 | tf_op jit(solution)/shard_map/convert_element_type | solution.py:17
  1.5 0.7 all_to_all.22
  2.1 5.2 %all-to-all-start = ((f32[8,4,1]{1,2,0:T(1,128)}), f32[8,4,1]{1,2,0:T(1,128)S(1)}, u32[]{:S(2)}, u32[]{:S(2)}) async-start(f32[8,4,1]{1,2,0:T(1,128)} %bitcast.1), calls=%async_computation | async-start | bytes 8192 | tf_op jit(solution)/shard_map/all_to_all | solution.py:16
  7.3 0.7 fusion.16
  8.1 0.1 reshape.35
  8.2 1.4 %multiply_bitcast_fusion = f32[4,8,128]{2,1,0:T(8,128)} fusion(f32[32,128]{1,0:T(8,128)} %param.11, f32[32]{0:T(128)S(1)} %reshape.35), kind=kLoop, calls=%fused_computation.21 | loop fusion | flops 4096 | bytes 32896 | tf_op jit(solution)/shard_map/all_to_all | solution.py:29
  9.5 2.8 %convolution_bitcast_fusion = f32[20,20]{1,0:T(8,128)S(1)} fusion(f32[20,64,128]{2,1,0:T(8,128)} %param.7), kind=kOutput, calls=%fused_computation.4 | convolution fusion | flops 39321600 | bytes 656960 | tf_op jit(solution)/shard_map/kfi,lfi->kl/dot_general | solution.py:38
  12.3 0.0 all-to-all-done
  12.3 4.2 %all-to-all-start.1 = ((f32[8,4,128]{2,1,0:T(4,128)}), f32[8,4,128]{2,1,0:T(4,128)S(1)}, u32[]{:S(2)}, u32[]{:S(2)}) async-start(f32[8,4,128]{2,1,0:T(4,128)} %bitcast.45), calls=%async_computation.1 | async-start | bytes 32768 | tf_op jit(solution)/shard_map/all_to_all | solution.py:15
  16.5 0.1 convert_element_type.31
  16.6 4.7 %all-to-all-done.1 = f32[8,4,128]{2,1,0:T(4,128)S(1)} async-done(((f32[8,4,128]{2,1,0:T(4,128)}), f32[8,4,128]{2,1,0:T(4,128)S(1)}, u32[]{:S(2)}, u32[]{:S(2)}) %all-to-all-start.1) | async-done | bytes 16416 | tf_op jit(solution)/shard_map/all_to_all | solution.py:15
  21.3 4.9 %all-to-all-start.2 = ((f32[4,8,128]{2,1,0:T(8,128)}), f32[4,8,128]{2,1,0:T(8,128)S(1)}, u32[]{:S(2)}, u32[]{:S(2)}) async-start(f32[4,8,128]{2,1,0:T(8,128)} %multiply_bitcast_fusion), calls=%async_computation.2 | async-start | bytes 32768 | tf_op jit(solution)/shard_map/all_to_all | solution.py:29
  26.2 0.9 %convolution_add_fusion.1 = f32[64,128]{1,0:T(8,128)S(1)} fusion(f32[32,128]{1,0:T(8,128)S(1)} %bitcast.44, f32[20,64,128]{2,1,0:T(8,128)} %param.7, s32[32]{0:T(128)S(1)} %convert_element_type.31), kind=kOutput, calls=%fused_computation.1 | convolution fusion | flops 3155968 | bytes 82048 | tf_op jit(solution)/shard_map/dot_general | solution.py:21
  27.1 4.7 %all-to-all-done.2 = f32[4,8,128]{2,1,0:T(8,128)S(1)} async-done(((f32[4,8,128]{2,1,0:T(8,128)}), f32[4,8,128]{2,1,0:T(8,128)S(1)}, u32[]{:S(2)}, u32[]{:S(2)}) %all-to-all-start.2) | async-done | bytes 16416 | tf_op jit(solution)/shard_map/all_to_all | solution.py:29
  31.8 0.8 %fusion.1 = bf16[64,128,1]{1,0,2:T(8,128)(2,1)S(1)} fusion(f32[64,128]{1,0:T(8,128)S(1)} %convolution_add_fusion.1, f32[4,8,128]{2,1,0:T(8,128)S(1)} %all-to-all-done.2, s32[32]{0:T(128)} %param.12), kind=kOutput, calls=%fused_computation.3 | convolution fusion | flops 3164160 | bytes 65664 | tf_op jit(solution)/shard_map/dot_general | solution.py:31
  32.6 0.0 copy-done
  32.6 1.2 %fusion.9 = f32[64,1,128]{2,1,0:T(1,128)S(1)} fusion(bf16[64,128,128]{2,1,0:T(8,128)(2,1)S(1)} %copy-done, bf16[64,128,1]{1,0,2:T(8,128)(2,1)S(1)} %fusion.1), kind=kOutput, calls=%fused_computation.14 | convolution fusion | flops 2097152 | bytes 2146304 | tf_op jit(solution)/shard_map/fij,fj->fi/dot_general | solution.py:35
  33.8 0.0 copy-done.1
  33.8 1.1 %convolution_bitcast_fusion.2 = f32[20]{0:T(128)S(1)} fusion(f32[20,64,128]{2,1,0:T(8,128)S(1)} %copy-done.1, f32[64,1,128]{2,1,0:T(1,128)S(1)} %fusion.9), kind=kOutput, calls=%fused_computation.7 | convolution fusion | flops 1966080 | bytes 688208 | tf_op jit(solution)/shard_map/kfi,fi->k/dot_general | solution.py:37
  34.8 0.6 multiply_reduce_fusion
  35.5 38.5 %all-reduce = (f32[]{:T(128)}, f32[20]{0:T(128)S(1)}, f32[20,20]{1,0:T(8,128)S(1)}) all-reduce(f32[]{:T(128)} %multiply_reduce_fusion, f32[20]{0:T(128)S(1)} %convolution_bitcast_fusion.2, f32[20,20]{1,0:T(8,128)S(1)} %convolution_bitcast_fusion), channel_id=1, replica_groups=mesh['grp'=4,'mem'=8] {'grp','mem'}, use_global_device_ids=true, to_apply=%region_2.0 | all-reduce | flops 421 | bytes 3368 | tf_op jit(solution)/shard_map/psum | solution.py:39
  74.0 0.6 broadcast_multiply_fusion
  74.6 0.9 %fusion.3 = f32[1,64,128]{2,0,1:T(1,128)S(1)} fusion(f32[20,64,128]{2,1,0:T(8,128)S(1)} %copy-done.1, f32[20]{0:T(128)S(1)} %get-tuple-element.3), kind=kOutput, calls=%fused_computation.8 | convolution fusion | flops 1966100 | bytes 688208 | tf_op jit(solution)/shard_map/k,kfi->fi/dot_general | solution.py:44
  75.5 0.8 %fusion.7 = f32[]{:T(128)} fusion(f32[20,20]{1,0:T(8,128)S(1)} %get-tuple-element.4, f32[20]{0:T(128)S(1)} %get-tuple-element.3), kind=kOutput, calls=%fused_computation.12 | convolution fusion | flops 5279 | bytes 1684 | tf_op jit(solution)/shard_map/dot_general | solution.py:45
  78.3 0.6 subtract_divide_fusion
  78.9 0.6 pad_maximum_fusion
  (1 shorter events, 0.0 us)
Async XLA Ops:
  0.6 31.9 %copy-start = (bf16[64,128,128]{2,1,0:T(8,128)(2,1)S(1)}, bf16[64,128,128]{2,1,0:T(8,128)(2,1)}, u32[]{:S(2)}) copy-start(bf16[64,128,128]{2,1,0:T(8,128)(2,1)} %param.8) | copy-start | bytes 6291460
  0.6 33.1 %copy-start.1 = (f32[20,64,128]{2,1,0:T(8,128)S(1)}, f32[20,64,128]{2,1,0:T(8,128)}, u32[]{:S(2)}) copy-start(f32[20,64,128]{2,1,0:T(8,128)} %param.7) | copy-start | bytes 1966084
  2.1 10.2 %all-to-all-start = ((f32[8,4,1]{1,2,0:T(1,128)}), f32[8,4,1]{1,2,0:T(1,128)S(1)}, u32[]{:S(2)}, u32[]{:S(2)}) async-start(f32[8,4,1]{1,2,0:T(1,128)} %bitcast.1), calls=%async_computation | async-start | bytes 8192 | tf_op jit(solution)/shard_map/all_to_all | solution.py:16
  12.3 9.0 %all-to-all-start.1 = ((f32[8,4,128]{2,1,0:T(4,128)}), f32[8,4,128]{2,1,0:T(4,128)S(1)}, u32[]{:S(2)}, u32[]{:S(2)}) async-start(f32[8,4,128]{2,1,0:T(4,128)} %bitcast.45), calls=%async_computation.1 | async-start | bytes 32768 | tf_op jit(solution)/shard_map/all_to_all | solution.py:15
  21.3 10.5 %all-to-all-start.2 = ((f32[4,8,128]{2,1,0:T(8,128)}), f32[4,8,128]{2,1,0:T(8,128)S(1)}, u32[]{:S(2)}, u32[]{:S(2)}) async-start(f32[4,8,128]{2,1,0:T(8,128)} %multiply_bitcast_fusion), calls=%async_computation.2 | async-start | bytes 32768 | tf_op jit(solution)/shard_map/all_to_all | solution.py:29
where the time goes:
time: 80.1 us; the launch traced here: 79.5 us
  blocking collectives  38.5 us (48%)
  starting transfers between devices  14.3 us (18%)
  waiting for transfers between devices  9.37 us (12%)
  matrix products  8.4 us (10%)
  other arithmetic  5.37 us (7%)
  between operations  2.73 us (3%)
  local copies, waits for them, and re-layouts  0.86 us (1%)
    psum x1, blocking collectives, local(): lax.psum((local_coef, jnp.sum(applied * applied), gram_local), ('grp', 'm...  38.5 us
    all_to_all x1, starting transfers between devices, local(): lax.all_to_all(leaf_fiber.astype(jnp.float32), 'mem', split_axis=0, conca...  5.2 us
    all_to_all x1, starting transfers between devices, local(): lax.all_to_all(outgoing, 'grp', split_axis=0, concat_axis=0, tiled=True)  4.88 us
    all_to_all x1, waiting for transfers between devices, local(): lax.all_to_all(outgoing, 'grp', split_axis=0, concat_axis=0, tiled=True)  4.71 us
    all_to_all x1, waiting for transfers between devices, local(): lax.all_to_all(leaf_rows, 'mem', split_axis=0, concat_axis=0, tiled=True)  4.65 us
    all_to_all x1, starting transfers between devices, local(): lax.all_to_all(leaf_rows, 'mem', split_axis=0, concat_axis=0, tiled=True)  4.21 us
    dot_general x1, matrix products, local(): jnp.einsum('kfi,lfi->kl', basis, basis, precision=lax.Precision.HIGHEST)  2.75 us
  transfers between devices with their start and end apart: 3, of which 2 were waited for; matrix products, arithmetic and copies ran while one was open for 7% of the time, Pallas kernels for 0%

commit v1 on v0

--- a/solution.py
+++ b/solution.py
@@ -37,7 +37,7 @@
     local_coef = jnp.einsum("kfi,fi->k", basis, applied, precision=lax.Precision.HIGHEST)
     gram_local = jnp.einsum("kfi,lfi->kl", basis, basis, precision=lax.Precision.HIGHEST)
     coef_sum, square_sum, gram_sum = lax.psum(
-        (local_coef, jnp.sum(applied * applied), gram_local), ("grp", "mem")
+        lax.psum((local_coef, jnp.sum(applied * applied), gram_local), "mem"), "grp"
     )
     coef = coef_sum / total
     gram = gram_sum / total

time: 80.1 us -> 82.1 us (1.025)
  blocking collectives: 38.5 us -> 40.5 us
    psum x1 -> x2, blocking collectives: 38.5 us -> 40.5 us  [the longest x1 23.4 us: local(): lax.psum((local_coef, jnp.sum(applied * applied), gram_local), 'mem')]
where the time goes in v1:
time: 82.1 us; the launch traced here: 81.5 us
  blocking collectives  40.5 us (49%)
  starting transfers between devices  14.3 us (17%)
  waiting for transfers between devices  9.37 us (11%)
  matrix products  8.4 us (10%)
  other arithmetic  5.37 us (7%)
  between operations  2.73 us (3%)
  local copies, waits for them, and re-layouts  0.86 us (1%)
    psum x1, blocking collectives, local(): lax.psum((local_coef, jnp.sum(applied * applied), gram_local), 'mem')  23.4 us
    psum x1, blocking collectives, local(): lax.psum(lax.psum((local_coef, jnp.sum(applied * applied), gram_local), '...  17.1 us
    all_to_all x1, starting transfers between devices, local(): lax.all_to_all(leaf_fiber.astype(jnp.float32), 'mem', split_axis=0, conca...  5.2 us
    all_to_all x1, starting transfers between devices, local(): lax.all_to_all(outgoing, 'grp', split_axis=0, concat_axis=0, tiled=True)  4.88 us
    all_to_all x1, waiting for transfers between devices, local(): lax.all_to_all(outgoing, 'grp', split_axis=0, concat_axis=0, tiled=True)  4.71 us
    all_to_all x1, waiting for transfers between devices, local(): lax.all_to_all(leaf_rows, 'mem', split_axis=0, concat_axis=0, tiled=True)  4.65 us
    all_to_all x1, starting transfers between devices, local(): lax.all_to_all(leaf_rows, 'mem', split_axis=0, concat_axis=0, tiled=True)  4.21 us
    dot_general x1, matrix products, local(): jnp.einsum('kfi,lfi->kl', basis, basis, precision=lax.Precision.HIGHEST)  2.75 us
  transfers between devices with their start and end apart: 3, of which 2 were waited for; matrix products, arithmetic and copies ran while one was open for 7% of the time, Pallas kernels for 0%

profile of v1, /device:TPU:0, one launch (start us, length us, event | category | flops | bytes accessed | tf_op | source)
XLA Modules:
  0.0 81.5 jit_solution(5662910104804222517)
XLA Ops:
  0.6 0.0 copy-start
  0.6 0.0 copy-start.1
  0.7 0.8 convert_element_type.29
  1.5 0.7 all_to_all.22
  2.1 5.2 %all-to-all-start = ((f32[8,4,1]{1,2,0:T(1,128)}), f32[8,4,1]{1,2,0:T(1,128)S(1)}, u32[]{:S(2)}, u32[]{:S(2)}) async-start(f32[8,4,1]{1,2,0:T(1,128)} %bitcast.1), calls=%async_computation | async-start | bytes 8192 | tf_op jit(solution)/shard_map/all_to_all | solution.py:16
  7.3 0.7 fusion.16
  8.1 0.1 reshape.35
  8.2 1.4 %multiply_bitcast_fusion = f32[4,8,128]{2,1,0:T(8,128)} fusion(f32[32,128]{1,0:T(8,128)} %param.11, f32[32]{0:T(128)S(1)} %reshape.35), kind=kLoop, calls=%fused_computation.21 | loop fusion | flops 4096 | bytes 32896 | tf_op jit(solution)/shard_map/all_to_all | solution.py:29
  9.5 2.8 %convolution_bitcast_fusion = f32[20,20]{1,0:T(8,128)S(1)} fusion(f32[20,64,128]{2,1,0:T(8,128)} %param.7), kind=kOutput, calls=%fused_computation.4 | convolution fusion | flops 39321600 | bytes 656960 | tf_op jit(solution)/shard_map/kfi,lfi->kl/dot_general | solution.py:38
  12.3 0.0 all-to-all-done
  12.3 4.2 %all-to-all-start.1 = ((f32[8,4,128]{2,1,0:T(4,128)}), f32[8,4,128]{2,1,0:T(4,128)S(1)}, u32[]{:S(2)}, u32[]{:S(2)}) async-start(f32[8,4,128]{2,1,0:T(4,128)} %bitcast.45), calls=%async_computation.1 | async-start | bytes 32768 | tf_op jit(solution)/shard_map/all_to_all | solution.py:15
  16.5 0.1 convert_element_type.31
  16.6 4.7 %all-to-all-done.1 = f32[8,4,128]{2,1,0:T(4,128)S(1)} async-done(((f32[8,4,128]{2,1,0:T(4,128)}), f32[8,4,128]{2,1,0:T(4,128)S(1)}, u32[]{:S(2)}, u32[]{:S(2)}) %all-to-all-start.1) | async-done | bytes 16416 | tf_op jit(solution)/shard_map/all_to_all | solution.py:15
  21.3 4.9 %all-to-all-start.2 = ((f32[4,8,128]{2,1,0:T(8,128)}), f32[4,8,128]{2,1,0:T(8,128)S(1)}, u32[]{:S(2)}, u32[]{:S(2)}) async-start(f32[4,8,128]{2,1,0:T(8,128)} %multiply_bitcast_fusion), calls=%async_computation.2 | async-start | bytes 32768 | tf_op jit(solution)/shard_map/all_to_all | solution.py:29
  26.2 0.9 %convolution_add_fusion.1 = f32[64,128]{1,0:T(8,128)S(1)} fusion(f32[32,128]{1,0:T(8,128)S(1)} %bitcast.44, f32[20,64,128]{2,1,0:T(8,128)} %param.7, s32[32]{0:T(128)S(1)} %convert_element_type.31), kind=kOutput, calls=%fused_computation.1 | convolution fusion | flops 3155968 | bytes 82048 | tf_op jit(solution)/shard_map/dot_general | solution.py:21
  27.1 4.7 %all-to-all-done.2 = f32[4,8,128]{2,1,0:T(8,128)S(1)} async-done(((f32[4,8,128]{2,1,0:T(8,128)}), f32[4,8,128]{2,1,0:T(8,128)S(1)}, u32[]{:S(2)}, u32[]{:S(2)}) %all-to-all-start.2) | async-done | bytes 16416 | tf_op jit(solution)/shard_map/all_to_all | solution.py:29
  31.8 0.8 fusion.1
  32.6 0.0 copy-done
  32.6 1.2 %fusion.9 = f32[64,1,128]{2,1,0:T(1,128)S(1)} fusion(bf16[64,128,128]{2,1,0:T(8,128)(2,1)S(1)} %copy-done, bf16[64,128,1]{1,0,2:T(8,128)(2,1)S(1)} %fusion.1), kind=kOutput, calls=%fused_computation.14 | convolution fusion | flops 2097152 | bytes 2146304 | tf_op jit(solution)/shard_map/fij,fj->fi/dot_general | solution.py:35
  33.8 0.0 copy-done.1
  33.8 1.1 %convolution_bitcast_fusion.2 = f32[20]{0:T(128)S(1)} fusion(f32[20,64,128]{2,1,0:T(8,128)S(1)} %copy-done.1, f32[64,1,128]{2,1,0:T(1,128)S(1)} %fusion.9), kind=kOutput, calls=%fused_computation.7 | convolution fusion | flops 1966080 | bytes 688208 | tf_op jit(solution)/shard_map/kfi,fi->k/dot_general | solution.py:37
  34.8 0.6 multiply_reduce_fusion
  35.5 23.4 %all-reduce = (f32[]{:T(128)}, f32[20]{0:T(128)S(1)}, f32[20,20]{1,0:T(8,128)S(1)}) all-reduce(f32[]{:T(128)} %multiply_reduce_fusion, f32[20]{0:T(128)S(1)} %convolution_bitcast_fusion.2, f32[20,20]{1,0:T(8,128)S(1)} %convolution_bitcast_fusion), channel_id=1, replica_groups=mesh['grp'=4,'mem'=8] {'mem'}, use_global_device_ids=true, to_apply=%region_3.0 | all-reduce | flops 421 | bytes 3368 | tf_op jit(solution)/shard_map/psum | solution.py:40
  58.8 17.1 %all-reduce.1 = (f32[]{:T(128)}, f32[20]{0:T(128)S(1)}, f32[20,20]{1,0:T(8,128)S(1)}) all-reduce(f32[]{:T(128)} %get-tuple-element.2, f32[20]{0:T(128)S(1)} %get-tuple-element.3, f32[20,20]{1,0:T(8,128)S(1)} %get-tuple-element.4), channel_id=1, replica_groups=mesh['grp'=4,'mem'=8] {'grp'}, use_global_device_ids=true, to_apply=%region_4.0 | all-reduce | flops 421 | bytes 3368 | tf_op jit(solution)/shard_map/psum | solution.py:39
  76.0 0.6 broadcast_multiply_fusion
  76.6 0.9 %fusion.3 = f32[1,64,128]{2,0,1:T(1,128)S(1)} fusion(f32[20,64,128]{2,1,0:T(8,128)S(1)} %copy-done.1, f32[20]{0:T(128)S(1)} %get-tuple-element.6), kind=kOutput, calls=%fused_computation.8 | convolution fusion | flops 1966100 | bytes 688208 | tf_op jit(solution)/shard_map/k,kfi->fi/dot_general | solution.py:44
  77.5 0.8 %fusion.7 = f32[]{:T(128)} fusion(f32[20,20]{1,0:T(8,128)S(1)} %get-tuple-element.7, f32[20]{0:T(128)S(1)} %get-tuple-element.6), kind=kOutput, calls=%fused_computation.12 | convolution fusion | flops 5279 | bytes 1684 | tf_op jit(solution)/shard_map/dot_general | solution.py:45
  80.3 0.6 subtract_divide_fusion
  80.9 0.6 pad_maximum_fusion
  (1 shorter events, 0.0 us)
Async XLA Ops:
  0.6 31.9 %copy-start = (bf16[64,128,128]{2,1,0:T(8,128)(2,1)S(1)}, bf16[64,128,128]{2,1,0:T(8,128)(2,1)}, u32[]{:S(2)}) copy-start(bf16[64,128,128]{2,1,0:T(8,128)(2,1)} %param.8) | copy-start | bytes 6291460
  0.6 33.1 %copy-start.1 = (f32[20,64,128]{2,1,0:T(8,128)S(1)}, f32[20,64,128]{2,1,0:T(8,128)}, u32[]{:S(2)}) copy-start(f32[20,64,128]{2,1,0:T(8,128)} %param.7) | copy-start | bytes 1966084
  2.1 10.2 %all-to-all-start = ((f32[8,4,1]{1,2,0:T(1,128)}), f32[8,4,1]{1,2,0:T(1,128)S(1)}, u32[]{:S(2)}, u32[]{:S(2)}) async-start(f32[8,4,1]{1,2,0:T(1,128)} %bitcast.1), calls=%async_computation | async-start | bytes 8192 | tf_op jit(solution)/shard_map/all_to_all | solution.py:16
  12.3 9.0 %all-to-all-start.1 = ((f32[8,4,128]{2,1,0:T(4,128)}), f32[8,4,128]{2,1,0:T(4,128)S(1)}, u32[]{:S(2)}, u32[]{:S(2)}) async-start(f32[8,4,128]{2,1,0:T(4,128)} %bitcast.45), calls=%async_computation.1 | async-start | bytes 32768 | tf_op jit(solution)/shard_map/all_to_all | solution.py:15
  21.3 10.5 %all-to-all-start.2 = ((f32[4,8,128]{2,1,0:T(8,128)}), f32[4,8,128]{2,1,0:T(8,128)S(1)}, u32[]{:S(2)}, u32[]{:S(2)}) async-start(f32[4,8,128]{2,1,0:T(8,128)} %multiply_bitcast_fusion), calls=%async_computation.2 | async-start | bytes 32768 | tf_op jit(solution)/shard_map/all_to_all | solution.py:29
